TPU v7x, 256 devices: a whole 4x4x8 slice. The times are simulated.
256 devices in a mesh: row: 16 (over x, z_lo, core), col: 16 (over y, z_hi).
Axes of the slice: x: 4, y: 4, z: 8 (z_hi: 4, z_lo: 2; z = z_hi * 2 + z_lo), core: 2. Of those that a mesh axis runs over, the one named last changes fastest.
Arguments:
- ancestor_inverse: bfloat16 [32768, 32768], P('row', 'col'), may hold values from -0.03125 to 0.03125
- panel: bfloat16 [32768, 512], P(('row', 'col')), may hold values from -0.75 to 0.75
- structure: int32 [2, 128], replicated, may hold values 0 or 1
- diag_inverse: float32 [2, 256, 256], replicated, may hold values from -6 to 6
Outputs:
- upper: bfloat16 [32768, 512], P(('row', 'col'))
- diagonal: float32 [2, 256, 256], replicated
All inputs are finite; a program needn't handle non-finite values.
Results may differ from a plain program's by a relative error of at most 0.0014.
Values may be sent and summed in bfloat16 or wider, within the bound.
A program may use at most 64 MiB of HBM per device.

v0:
```python
import jax
import jax.numpy as jnp
from jax import lax
from jax.sharding import PartitionSpec as P


def from_root(block, axis, source):
    block = jnp.where(lax.axis_index(axis) == source, block, jnp.zeros_like(block))
    return lax.psum(block, axis)


def row_keep(begin_row, length, structure, blk_width):
    blocks_all = structure.shape[1]
    indices = begin_row + jnp.arange(length, dtype=jnp.int32)
    owners = indices // blk_width
    onehot = (owners[:, None] == jnp.arange(blocks_all, dtype=jnp.int32)[None, :]).astype(
        jnp.float32
    )
    keeps = jnp.dot(onehot, structure.T.astype(jnp.float32), preferred_element_type=jnp.float32)
    return jnp.repeat(keeps, blk_width, axis=1)


def diag_part(lower, upper_rows, blk_width):
    snodes = upper_rows.shape[1] // blk_width
    lower_f = lower.astype(jnp.float32).reshape(lower.shape[0], snodes, blk_width)
    upper_f = upper_rows.reshape(upper_rows.shape[0], snodes, blk_width)
    return jnp.einsum("mkw,mkv->kwv", lower_f, upper_f, precision=lax.Precision.HIGHEST)


def local(ancestor_inverse, panel, structure, diag_inverse):
    blk_width = diag_inverse.shape[1]
    row_count = lax.axis_size("row")
    col_count = lax.axis_size("col")
    row_index = lax.axis_index("row")
    col_index = lax.axis_index("col")
    piece_rows = panel.shape[0]
    begin_own = (row_index * col_count + col_index) * piece_rows
    keep_own = row_keep(begin_own, piece_rows, structure, blk_width)
    masked = panel * keep_own.astype(jnp.bfloat16)
    row_block = lax.all_gather(masked, "col", axis=0, tiled=True)
    ratio = col_count // row_count
    root_row = col_index // ratio
    col_block = from_root(row_block, "row", root_row)
    partial_rows = -jnp.dot(ancestor_inverse, col_block, preferred_element_type=jnp.float32)
    full_rows = lax.psum(partial_rows, "col")
    own_rows = lax.dynamic_slice_in_dim(full_rows, col_index * piece_rows, piece_rows, 0)
    diag_sum = lax.psum(diag_part(masked, own_rows, blk_width), ("row", "col"))
    upper = (own_rows * keep_own).astype(jnp.bfloat16)
    diagonal = diag_inverse - diag_sum
    return (upper, diagonal)


def solution(mesh):
    return jax.shard_map(
        local,
        mesh=mesh,
        in_specs=(P("row", "col"), P(("row", "col"), None), P(), P()),
        out_specs=(P(("row", "col"), None), P()),
        check_vma=False,
    )
```

profile of v0, /device:TPU:1, one launch (start us, length us, event | category | flops | bytes accessed | tf_op | source)
XLA Modules:
  0.0 704.2 jit_solution(14977769221147062847)
XLA Ops:
  7.2 0.0 all-gather.2.cloned.1.call-start
  7.2 1.0 copy.8
  8.3 0.9 fusion.2
  9.1 0.7 fusion.1
  9.8 0.0 all-gather.2.cloned.1.call-update
  9.9 0.0 all-reduce.4.cloned.1.call-start
  9.9 66.3 %all-gather.2.cloned.1.call-done = bf16[2048,512]{0,1:T(8,128)(2,1)} async-done(((bf16[128,512]{0,1:T(8,128)(2,1)}), bf16[2048,512]{0,1:T(8,128)(2,1)}) %all-gather.2.cloned.1.call-update) | async-done | bytes 2097168 | tf_op jit(solution)/shard_map/all_gather | solution.py:40
  76.3 1.5 broadcast_select_fusion
  77.8 0.0 all-reduce.4.cloned.1.call-update
  77.8 0.0 all-reduce.6.cloned.1.call-start
  77.8 128.4 %all-reduce.4.cloned.1.call-done = bf16[2048,512]{0,1:T(8,128)(2,1)} async-done(((bf16[2048,512]{0,1:T(8,128)(2,1)}), bf16[2048,512]{0,1:T(8,128)(2,1)}) %all-reduce.4.cloned.1.call-update) | async-done | bytes 2097168 | tf_op jit(solution)/shard_map/psum | solution.py:9
  206.2 10.5 %negate_bitcast_fusion = f32[2048,512]{0,1:T(8,128)} fusion(bf16[2048,512]{0,1:T(8,128)(2,1)} %all-reduce.4.cloned.1.call-done, bf16[2048,2048]{1,0:T(8,128)(2,1)} %param.4), kind=kOutput, calls=%fused_computation | convolution fusion | flops 4296015872 | bytes 14680064 | tf_op jit(solution)/shard_map/dot_general | solution.py:44
  216.7 0.0 copy-start
  216.7 0.0 copy-start.1
  216.7 0.0 all-reduce.6.cloned.1.call-update
  216.8 0.0 all-reduce.8.cloned.1.call-start
  216.8 217.0 %all-reduce.6.cloned.1.call-done = f32[2048,512]{0,1:T(8,128)} async-done(((f32[2048,512]{0,1:T(8,128)}), f32[2048,512]{0,1:T(8,128)}) %all-reduce.6.cloned.1.call-update) | async-done | bytes 4194320 | tf_op jit(solution)/shard_map/psum | solution.py:45
  433.8 1.0 fusion
  434.8 0.0 copy-done
  434.8 1.2 fusion.5
  436.0 0.0 all-reduce.8.cloned.1.call-update
  436.0 0.8 copy.10
  436.8 259.0 %all-reduce.8.cloned.1.call-done = f32[2,256,256]{2,1,0:T(8,128)} async-done(((f32[2,256,256]{2,1,0:T(8,128)}), f32[2,256,256]{2,1,0:T(8,128)}) %all-reduce.8.cloned.1.call-update) | async-done | bytes 524304 | tf_op jit(solution)/shard_map/psum | solution.py:47
  695.8 0.0 copy-done.1
  695.8 1.9 sub.12
  (1 shorter events, 0.0 us)
Async XLA Ops:
  7.2 69.1 %all-gather.2.cloned.1.call-start = ((), (), s32[]{:S(2)}) async-start(), calls=%async_computation | async-start | bytes 2228224 | tf_op jit(solution)/shard_map/all_gather | solution.py:40
  9.9 196.4 %all-reduce.4.cloned.1.call-start = ((), (), s32[]{:S(2)}) async-start(), calls=%async_computation.1 | async-start | bytes 4194304 | tf_op jit(solution)/shard_map/psum | solution.py:9
  77.8 356.0 %all-reduce.6.cloned.1.call-start = ((), (), s32[]{:S(2)}) async-start(), calls=%async_computation.2 | async-start | bytes 8388608 | tf_op jit(solution)/shard_map/psum | solution.py:45
  216.7 218.0 %copy-start = (bf16[128,512]{0,1:T(8,128)(2,1)S(1)}, bf16[128,512]{0,1:T(8,128)(2,1)}, u32[]{:S(2)}) copy-start(bf16[128,512]{0,1:T(8,128)(2,1)} %fusion.1) | copy-start | bytes 393220
  216.7 479.0 %copy-start.1 = (f32[2,256,256]{2,1,0:T(8,128)S(1)}, f32[2,256,256]{2,1,0:T(8,128)}, u32[]{:S(2)}) copy-start(f32[2,256,256]{2,1,0:T(8,128)} %param.7) | copy-start | bytes 1572868
  216.8 479.0 %all-reduce.8.cloned.1.call-start = ((), (), s32[]{:S(2)}) async-start(), calls=%async_computation.3 | async-start | bytes 1048576 | tf_op jit(solution)/shard_map/psum | solution.py:47
Sparse Core Ops, SparseCore 0:
  10.9 65.2 all-gather.1
  78.9 127.2 all-reduce.3
  216.9 216.8 all-reduce.5
  439.7 256.0 all-reduce.7
where the time goes:
time: 705 us; the launch traced here: 704 us
  waiting for transfers between devices  671 us (95%)
  between operations  13.8 us (2%)
  matrix products  12.6 us (2%)
    psum x1, waiting for transfers between devices, local(): diag_sum = lax.psum(diag_part(masked, own_rows, blk_width), ('row', 'col'))  259 us
    psum x1, waiting for transfers between devices, local(): full_rows = lax.psum(partial_rows, 'col')  217 us
    psum x1, waiting for transfers between devices, from_root(): return lax.psum(block, axis)  128 us
    all_gather x1, waiting for transfers between devices, local(): row_block = lax.all_gather(masked, 'col', axis=0, tiled=True)  66.3 us
  transfers between devices with their start and end apart: 4, of which 4 were waited for; matrix products, arithmetic and copies ran while one was open for 0% of the time, Pallas kernels for 0%

commit v1 on v0

--- a/solution.py
+++ b/solution.py
@@ -2,11 +2,6 @@
 import jax.numpy as jnp
 from jax import lax
 from jax.sharding import PartitionSpec as P
-
-
-def from_root(block, axis, source):
-    block = jnp.where(lax.axis_index(axis) == source, block, jnp.zeros_like(block))
-    return lax.psum(block, axis)
 
 
 def row_keep(begin_row, length, structure, blk_width):
@@ -37,13 +32,11 @@
     begin_own = (row_index * col_count + col_index) * piece_rows
     keep_own = row_keep(begin_own, piece_rows, structure, blk_width)
     masked = panel * keep_own.astype(jnp.bfloat16)
-    row_block = lax.all_gather(masked, "col", axis=0, tiled=True)
-    ratio = col_count // row_count
-    root_row = col_index // ratio
-    col_block = from_root(row_block, "row", root_row)
+    flip = [(r * col_count + c, c * row_count + r) for r in range(row_count) for c in range(col_count)]
+    moved = lax.ppermute(masked, ("row", "col"), flip)
+    col_block = lax.all_gather(moved, "row", axis=0, tiled=True)
     partial_rows = -jnp.dot(ancestor_inverse, col_block, preferred_element_type=jnp.float32)
-    full_rows = lax.psum(partial_rows, "col")
-    own_rows = lax.dynamic_slice_in_dim(full_rows, col_index * piece_rows, piece_rows, 0)
+    own_rows = lax.psum_scatter(partial_rows, "col", scatter_dimension=0, tiled=True)
     diag_sum = lax.psum(diag_part(masked, own_rows, blk_width), ("row", "col"))
     upper = (own_rows * keep_own).astype(jnp.bfloat16)
     diagonal = diag_inverse - diag_sum

time: 705 us -> 442 us (0.63)
  waiting for transfers between devices: 671 us -> 402 us
    psum x2 -> x0, waiting for transfers between devices: 345 us -> none  [the longest x1 217 us: local(): full_rows = lax.psum(partial_rows, 'col')]
    reduce_scatter x0 -> x1, waiting for transfers between devices: none -> 95.8 us  [local(): lax.psum_scatter(partial_rows, 'col', scatter_dimension=0, tiled=True)]
    all_gather x1, waiting for transfers between devices: 66.3 us -> 48.6 us  [local(): col_block = lax.all_gather(moved, 'row', axis=0, tiled=True)]
where the time goes in v1:
time: 442 us; the launch traced here: 441 us
  waiting for transfers between devices  402 us (91%)
  between operations  13.8 us (3%)
  matrix products  13.5 us (3%)
  starting transfers between devices  6.4 us (1%)
    psum x1, waiting for transfers between devices, local(): diag_sum = lax.psum(diag_part(masked, own_rows, blk_width), ('row', 'col'))  255 us
    reduce_scatter x1, waiting for transfers between devices, local(): lax.psum_scatter(partial_rows, 'col', scatter_dimension=0, tiled=True)  95.8 us
    all_gather x1, waiting for transfers between devices, local(): col_block = lax.all_gather(moved, 'row', axis=0, tiled=True)  48.6 us
    dot_general x1, matrix products, local(): jnp.dot(ancestor_inverse, col_block, preferred_element_type=jnp.float32)  10.5 us
  transfers between devices with their start and end apart: 4, of which 4 were waited for; matrix products, arithmetic and copies ran while one was open for 0% of the time, Pallas kernels for 0%

profile of v1, /device:TPU:1, one launch (start us, length us, event | category | flops | bytes accessed | tf_op | source)
XLA Modules:
  0.0 441.5 jit_solution(1587222471581334880)
XLA Ops:
  7.2 0.0 all-gather.2.cloned.1.call-start
  7.2 1.0 copy.6
  8.3 0.9 fusion.2
  9.2 6.3 %collective-permute-start = (bf16[128,512]{0,1:T(8,128)(2,1)S(1)}, bf16[128,512]{0,1:T(8,128)(2,1)S(1)}, u32[]{:S(2)}, u32[]{:S(2)}) collective-permute-start(bf16[128,512]{0,1:T(8,128)(2,1)S(1)} %fusion.1), channel_id=1, source_target_pairs={{0,0},{1,16},{2,32},{3,48},{4,64},{5,80},{6,96},{7,112},{8,128},{9... | collective-permute-start | bytes 393224 | tf_op jit(solution)/shard_map/ppermute | solution.py:36
  15.5 2.6 collective-permute-done
  18.1 0.0 copy-start.1
  18.1 0.7 copy-done.1
  18.8 0.0 all-gather.2.cloned.1.call-update
  18.8 0.0 reduce-scatter.2.cloned.1.call-start
  18.8 48.6 %all-gather.2.cloned.1.call-done = bf16[2048,512]{0,1:T(8,128)(2,1)} async-done(((bf16[128,512]{0,1:T(8,128)(2,1)}), bf16[2048,512]{0,1:T(8,128)(2,1)}) %all-gather.2.cloned.1.call-update) | async-done | bytes 2097168 | tf_op jit(solution)/shard_map/all_gather | solution.py:37
  67.5 10.5 %negate_bitcast_fusion = f32[2048,512]{0,1:T(8,128)} fusion(bf16[2048,512]{0,1:T(8,128)(2,1)} %all-gather.2.cloned.1.call-done, bf16[2048,2048]{1,0:T(8,128)(2,1)} %param.4), kind=kOutput, calls=%fused_computation | convolution fusion | flops 4296015872 | bytes 14680064 | tf_op jit(solution)/shard_map/dot_general | solution.py:38
  78.0 0.0 copy-start
  78.0 0.0 reduce-scatter.2.cloned.1.call-update
  78.0 0.0 all-reduce.2.cloned.1.call-start
  78.0 95.8 %reduce-scatter.2.cloned.1.call-done = f32[128,512]{0,1:T(8,128)} async-done(((f32[2048,512]{0,1:T(8,128)}), f32[128,512]{0,1:T(8,128)}) %reduce-scatter.2.cloned.1.call-update) | async-done | bytes 262160 | tf_op jit(solution)/shard_map/reduce_scatter | solution.py:39
  173.9 2.1 fusion.5
  176.0 0.0 all-reduce.2.cloned.1.call-update
  176.0 1.0 fusion
  177.0 0.8 copy.8
  177.8 255.2 %all-reduce.2.cloned.1.call-done = f32[2,256,256]{2,1,0:T(8,128)} async-done(((f32[2,256,256]{2,1,0:T(8,128)}), f32[2,256,256]{2,1,0:T(8,128)}) %all-reduce.2.cloned.1.call-update) | async-done | bytes 524304 | tf_op jit(solution)/shard_map/psum | solution.py:40
  433.0 0.0 copy-done
  433.0 1.9 sub.10
  (2 shorter events, 0.0 us)
Async XLA Ops:
  7.2 60.3 %all-gather.2.cloned.1.call-start = ((), (), s32[]{:S(2)}) async-start(), calls=%async_computation.1 | async-start | bytes 2228224 | tf_op jit(solution)/shard_map/all_gather | solution.py:37
  9.2 8.9 %collective-permute-start = (bf16[128,512]{0,1:T(8,128)(2,1)S(1)}, bf16[128,512]{0,1:T(8,128)(2,1)S(1)}, u32[]{:S(2)}, u32[]{:S(2)}) collective-permute-start(bf16[128,512]{0,1:T(8,128)(2,1)S(1)} %fusion.1), channel_id=1, source_target_pairs={{0,0},{1,16},{2,32},{3,48},{4,64},{5,80},{6,96},{7,112},{8,128},{9... | collective-permute-start | bytes 393224 | tf_op jit(solution)/shard_map/ppermute | solution.py:36
  18.1 0.7 copy-start.1
  18.8 155.1 %reduce-scatter.2.cloned.1.call-start = ((), (), s32[]{:S(2)}) async-start(), calls=%async_computation.2 | async-start | bytes 4456448 | tf_op jit(solution)/shard_map/reduce_scatter | solution.py:39
  78.0 355.0 %copy-start = (f32[2,256,256]{2,1,0:T(8,128)S(1)}, f32[2,256,256]{2,1,0:T(8,128)}, u32[]{:S(2)}) copy-start(f32[2,256,256]{2,1,0:T(8,128)} %param.7) | copy-start | bytes 1572868
  78.0 355.0 %all-reduce.2.cloned.1.call-start = ((), (), s32[]{:S(2)}) async-start(), calls=%async_computation.3 | async-start | bytes 1048576 | tf_op jit(solution)/shard_map/psum | solution.py:40
Sparse Core Ops, SparseCore 0:
  18.9 48.5 all-gather.1
  78.1 95.7 reduce-scatter.1
  179.9 253.0 all-reduce.1

commit v2 on v1

v2 whole, which is shorter than its diff:
```python
import functools

import jax
import jax.numpy as jnp
from jax import lax
from jax.experimental import pallas as pl
from jax.experimental.pallas import tpu as pltpu
from jax.sharding import PartitionSpec as P

MESH = pl.DeviceIdType.MESH
F32 = jnp.float32
BF16 = jnp.bfloat16
I16 = jnp.int16
WIDE = 256
PIECE = 128
ROUND = 12582912.0


def encode(tile, ref):
    rows = tile.shape[0]
    top = jnp.maximum(jnp.max(jnp.abs(tile), axis=0, keepdims=True), 1e-30)
    power = jnp.floor(jnp.log2(top)) - 13.0
    scaled = tile * jnp.exp2(-power)
    whole = (scaled + ROUND) - ROUND
    ref[0:rows, :] = whole.astype(jnp.int32).astype(I16)
    ref[rows:rows + 16, :] = jnp.broadcast_to(power, (16, tile.shape[1])).astype(jnp.int32).astype(I16)


def decode(ref, first=0, count=None):
    rows = ref.shape[0] - 16
    count = rows if count is None else count
    power = ref[rows:rows + 16, :].astype(jnp.int32).astype(F32)
    scale = jnp.exp2(power)[0:1, :]
    return ref[first:first + count, :].astype(jnp.int32).astype(F32) * scale


def kernel(a_hbm, panel_ref, structure_ref, dinv_hbm, upper_ref, diag_ref,
           a_v, own, neg, xb, sy, ry, sz, rz, ss, dsend, drecv, xs, xr, ys, yr, zr,
           dg, dchunk, lsem, ssem, rsem):
    R = lax.axis_index("row")
    C = lax.axis_index("col")
    x, zl, k = R // 4, (R // 2) % 2, R % 2
    y, zh = C // 4, C % 4
    z = zh * 2 + zl

    def at(dx=0, dy=0, dz=0, dzh=0, flip=False, sib=False):
        x2 = (x + dx) % 4
        y2 = (y + dy) % 4
        z2 = (z + dz + 2 * dzh) % 8
        zl2 = 1 - z2 % 2 if flip else z2 % 2
        k2 = 1 - k if sib else k
        return (x2 * 4 + zl2 * 2 + k2, y2 * 4 + z2 // 2)

    off_diagonal = R != C
    ids = {}
    sends = []

    def copy(name, src, dst, dev):
        i = ids.setdefault(name, len(ids))
        return pltpu.make_async_remote_copy(
            src_ref=src, dst_ref=dst, send_sem=ssem.at[i], recv_sem=rsem.at[i],
            device_id=dev, device_id_type=MESH)

    def send(name, src, dst, dev):
        cp = copy(name, src, dst, dev)
        cp.start()
        sends.append(cp)

    def recv(name, dst):
        copy(name, dst, dst, at(sib=True)).wait_recv()

    loads = []
    for t in range(8):
        cp = pltpu.make_async_copy(a_hbm.at[pl.ds(t * 256, 256), :], a_v.at[pl.ds(t * 256, 256), :], lsem.at[t])
        cp.start()
        loads.append(cp)
    mine16 = pl.multiple_of(x * 64 + y * 16, 16)
    cp = pltpu.make_async_copy(dinv_hbm.at[k, pl.ds(mine16, 16), :], dchunk, lsem.at[8])
    cp.start()
    loads.append(cp)

    block = (R * 16 + C) // 2
    keeps = []
    for q in range(2):
        keep = structure_ref[q, block].astype(F32)
        keeps.append(keep)
        m = panel_ref[:, q * WIDE:(q + 1) * WIDE].astype(F32) * keep
        own[q] = m.astype(BF16)
        neg[q] = (-m).astype(BF16)

    barrier = pltpu.get_barrier_semaphore()
    partners = [at(sib=True)]
    partners += [at(dx=d) for d in (1, 2, 3)]
    partners += [at(dy=d) for d in (1, 2, 3)]
    partners += [at(dz=d) for d in range(1, 8)]
    for dev in partners:
        pl.semaphore_signal(barrier, inc=1, device_id=dev, device_id_type=MESH)

    @pl.when(off_diagonal)
    def _():
        pl.semaphore_signal(barrier, inc=1, device_id=(C, R), device_id_type=MESH)
        pl.semaphore_wait(barrier, len(partners) + 1)

    @pl.when(jnp.logical_not(off_diagonal))
    def _():
        pl.semaphore_wait(barrier, len(partners))

    def slot(q, s):
        return xb.at[q, pl.ds(pl.multiple_of(s * PIECE, PIECE), PIECE), :]

    def half(q, s, h):
        return xb.at[q, pl.ds(pl.multiple_of(s * PIECE + h * 64, 64), 64), :]

    def lane(dx, n):
        return ((x + dx) % 4) * 4 + (zl + n) % 2 * 2 + k

    for q in range(2):
        first = copy(("g1", q), neg.at[q], slot(q, C), (C, R))

        @pl.when(off_diagonal)
        def _():
            first.start()

        @pl.when(jnp.logical_not(off_diagonal))
        def _():
            xb[q, pl.ds(pl.multiple_of(R * PIECE, PIECE), PIECE), :] = neg[q]

    def spread(q, n, s, dxs, i):
        if 1 in dxs:
            send(("gxp", q, n), slot(q, s), slot(q, s), at(dx=1))
        if -1 in dxs:
            send(("gxm", q, n), slot(q, s), slot(q, s), at(dx=-1))
        send(("gs", q, i), slot(q, s), slot(q, s), at(sib=True))

    def s1(q):
        @pl.when(off_diagonal)
        def _():
            recv(("g1", q), slot(q, R))
        send(("gz", q), slot(q, R), slot(q, R), at(flip=True))
        spread(q, 0, lane(0, 0), (1, -1), 0)

    def s2(q):
        recv(("gz", q), slot(q, lane(0, 1)))
        spread(q, 1, lane(0, 1), (1, -1), 1)

    def s3(q, n):
        s = lane(1, n)
        recv(("gxm", q, n), slot(q, s))
        send(("ghm", q, n), half(q, s, 0), half(q, s, 0), at(dx=-1))
        spread(q, n, s, (), 2 + n)
        s = lane(-1, n)
        recv(("gxp", q, n), slot(q, s))
        send(("ghp", q, n), half(q, s, 1), half(q, s, 1), at(dx=1))
        spread(q, n, s, (), 4 + n)

    def s5(q, n):
        s = lane(2, n)
        recv(("ghm", q, n), half(q, s, 0))
        recv(("ghp", q, n), half(q, s, 1))
        spread(q, n, s, (), 6 + n)

    def s6(q):
        for n in range(2):
            for i, dx in ((0, 0), (2, 1), (4, -1), (6, 2)):
                s = ((x + dx) % 4) * 4 + (zl + n) % 2 * 2 + 1 - k
                recv(("gs", q, i + n), slot(q, s))

    def tile(q, dy, u):
        r0 = pl.multiple_of(((y + dy) % 4) * 512 + u * 256, 256)
        return jnp.dot(a_v[pl.ds(r0, 256), :], xb[q], preferred_element_type=F32)

    def y_send(q, i, value, dy):
        encode(value, sy.at[q, i])
        send(("y", q, i), sy.at[q, i], ry.at[q, i], at(dy=dy))

    def y_first(q, after):
        y_send(q, 0, tile(q, 2, 0), 1)
        after(0)
        y_send(q, 1, tile(q, 2, 1), -1)
        after(1)
        y_send(q, 2, tile(q, 1, 1), 1)
        y_send(q, 3, tile(q, -1, 0), -1)

    def y_own(q):
        for u in range(2):
            ss[q, u * 256:(u + 1) * 256, :] = tile(q, 0, u)

    def y_relay(q):
        t = tile(q, 1, 0)
        recv(("y", q, 0), ry.at[q, 0])
        y_send(q, 4, t + decode(ry.at[q, 0]), 1)
        t = tile(q, -1, 1)
        recv(("y", q, 1), ry.at[q, 1])
        y_send(q, 5, t + decode(ry.at[q, 1]), -1)

    def y_last(q):
        for i in (2, 3, 4, 5):
            recv(("y", q, i), ry.at[q, i])
        ss[q, 0:256, :] = ss[q, 0:256, :] + decode(ry.at[q, 3]) + decode(ry.at[q, 4])
        ss[q, 256:512, :] = ss[q, 256:512, :] + decode(ry.at[q, 2]) + decode(ry.at[q, 5])

    def z_ref(buf, q, i):
        return buf.at[q, i, pl.ds(0, 80 if i < 2 else 144), :]

    def z_send(q, i, value, dzh):
        encode(value, z_ref(sz, q, i))
        send(("z", q, i), z_ref(sz, q, i), z_ref(rz, q, i), at(dzh=dzh))

    def z_rows(q, d, start, count):
        r0 = pl.multiple_of(((zh + d) % 4) * PIECE + start, 64)
        return ss[q, pl.ds(r0, count), :]

    def z_first(q):
        z_send(q, 0, z_rows(q, 2, 0, 64), 1)
        z_send(q, 1, z_rows(q, 2, 64, 64), -1)

    def z_relay(q):
        recv(("z", q, 0), z_ref(rz, q, 0))
        v = jnp.concatenate([z_rows(q, 1, 0, 64) + decode(z_ref(rz, q, 0)), z_rows(q, 1, 64, 64)], axis=0)
        z_send(q, 2, v, 1)
        recv(("z", q, 1), z_ref(rz, q, 1))
        v = jnp.concatenate([z_rows(q, -1, 0, 64), z_rows(q, -1, 64, 64) + decode(z_ref(rz, q, 1))], axis=0)
        z_send(q, 3, v, -1)

    def z_last(q):
        recv(("z", q, 2), z_ref(rz, q, 2))
        recv(("z", q, 3), z_ref(rz, q, 3))
        full = z_rows(q, 0, 0, PIECE) + decode(z_ref(rz, q, 2)) + decode(z_ref(rz, q, 3))
        upper_ref[:, q * WIDE:(q + 1) * WIDE] = (full * keeps[q]).astype(BF16)
        high = full.astype(BF16)
        low = (full - high.astype(F32)).astype(BF16)
        dims = (((0,), (0,)), ((), ()))
        dsend[q] = (lax.dot_general(own[q], high, dims, preferred_element_type=F32)
                    + lax.dot_general(own[q], low, dims, preferred_element_type=F32))

    s1(0)
    s1(1)
    s2(0)
    s3(0, 0)
    s2(1)
    s3(1, 0)
    s3(0, 1)
    s5(0, 0)
    s3(1, 1)
    s5(0, 1)
    s5(1, 0)
    for cp in loads:
        cp.wait()
    s6(0)

    def between(i):
        if i == 0:
            s5(1, 1)

    y_first(0, between)
    y_own(0)
    y_relay(0)
    s6(1)
    y_first(1, lambda i: None)
    y_own(1)
    y_last(0)
    z_first(0)
    y_relay(1)
    z_relay(0)
    z_last(0)
    y_last(1)
    z_first(1)
    z_relay(1)
    z_last(1)

    mate = at(sib=True)
    send("core", dsend.at[1 - k], drecv, mate)
    recv("core", drecv)
    xs[...] = dsend[k] + drecv[...]
    for d in (1, 2, 3):
        send(("dx", d), xs.at[pl.ds(pl.multiple_of(((x + d) % 4) * 64, 64), 64), :], xr.at[d - 1], at(dx=d))
    total = xs[pl.ds(pl.multiple_of(x * 64, 64), 64), :]
    for d in (1, 2, 3):
        recv(("dx", d), xr.at[d - 1])
        total = total + xr[d - 1]
    ys[...] = total
    for d in (1, 2, 3):
        send(("dy", d), ys.at[pl.ds(pl.multiple_of(((y + d) % 4) * 16, 16), 16), :], yr.at[d - 1], at(dy=d))
    total = ys[pl.ds(pl.multiple_of(y * 16, 16), 16), :]
    for d in (1, 2, 3):
        recv(("dy", d), yr.at[d - 1])
        total = total + yr[d - 1]
    zr[z] = total
    for d in range(1, 8):
        send(("dz", d), zr.at[z], zr.at[z], at(dz=d))
    for d in range(1, 8):
        recv(("dz", d), zr.at[(z + 8 - d) % 8])
    total = zr[0]
    for i in range(1, 8):
        total = total + zr[i]
    part = dg.at[k, pl.ds(mine16, 16), :]
    dg[k, pl.ds(mine16, 16), :] = dchunk[...] - total
    for d in (1, 2, 3):
        send(("ay", d), part, part, at(dy=d))
    for d in (1, 2, 3):
        recv(("ay", d), dg.at[k, pl.ds(pl.multiple_of(x * 64 + ((y + 4 - d) % 4) * 16, 16), 16), :])
    part = dg.at[k, pl.ds(pl.multiple_of(x * 64, 64), 64), :]
    for d in (1, 2, 3):
        send(("ax", d), part, part, at(dx=d))
    for d in (1, 2, 3):
        recv(("ax", d), dg.at[k, pl.ds(pl.multiple_of(((x + 4 - d) % 4) * 64, 64), 64), :])
    send("ac", dg.at[k], dg.at[k], mate)
    recv("ac", dg.at[1 - k])
    diag_ref[...] = dg[...]

    for q in range(2):
        cp = copy(("g1", q), neg.at[q], slot(q, C), (C, R))

        @pl.when(off_diagonal)
        def _():
            cp.wait_send()
    for cp in sends:
        cp.wait_send()
    assert len(ids) <= COPIES, len(ids)


COPIES = 96


def local(ancestor_inverse, panel, structure, diag_inverse):
    vmem = pl.BlockSpec(memory_space=pltpu.VMEM)
    hbm = pl.BlockSpec(memory_space=pl.ANY)
    return pl.pallas_call(
        kernel,
        out_shape=(jax.ShapeDtypeStruct(panel.shape, BF16), jax.ShapeDtypeStruct(diag_inverse.shape, F32)),
        in_specs=[hbm, vmem, pl.BlockSpec(memory_space=pltpu.SMEM), hbm],
        out_specs=(vmem, vmem),
        scratch_shapes=[
            pltpu.VMEM((2048, 2048), BF16),
            pltpu.VMEM((2, PIECE, WIDE), BF16),
            pltpu.VMEM((2, PIECE, WIDE), BF16),
            pltpu.VMEM((2, 2048, WIDE), BF16),
            pltpu.VMEM((2, 6, 272, WIDE), I16),
            pltpu.VMEM((2, 6, 272, WIDE), I16),
            pltpu.VMEM((2, 4, 144, WIDE), I16),
            pltpu.VMEM((2, 4, 144, WIDE), I16),
            pltpu.VMEM((2, 512, WIDE), F32),
            pltpu.VMEM((2, WIDE, WIDE), F32),
            pltpu.VMEM((WIDE, WIDE), F32),
            pltpu.VMEM((WIDE, WIDE), F32),
            pltpu.VMEM((3, 64, WIDE), F32),
            pltpu.VMEM((64, WIDE), F32),
            pltpu.VMEM((3, 16, WIDE), F32),
            pltpu.VMEM((8, 16, WIDE), F32),
            pltpu.VMEM((2, WIDE, WIDE), F32),
            pltpu.VMEM((16, WIDE), F32),
            pltpu.SemaphoreType.DMA((9,)),
            pltpu.SemaphoreType.DMA((COPIES,)),
            pltpu.SemaphoreType.DMA((COPIES,)),
        ],
        compiler_params=pltpu.CompilerParams(
            collective_id=0, has_side_effects=True, vmem_limit_bytes=60 * 1024 * 1024),
    )(ancestor_inverse, panel, structure, diag_inverse)


def solution(mesh):
    return jax.shard_map(
        local,
        mesh=mesh,
        in_specs=(P("row", "col"), P(("row", "col"), None), P(), P()),
        out_specs=(P(("row", "col"), None), P()),
        check_vma=False,
    )
```

time: 442 us -> 98.8 us (0.22)
  waiting for transfers between devices: 402 us -> 0 us
  Pallas kernels: 0 us -> 94.6 us
  matrix products: 13.5 us -> 0 us
  between operations: 13.8 us -> 0.64 us
  starting transfers between devices: 6.4 us -> 0 us
    psum x1 -> x0, waiting for transfers between devices: 255 us -> none  [local(): diag_sum = lax.psum(diag_part(masked, own_rows, blk_width), ('row', 'col'))]
    reduce_scatter x1 -> x0, waiting for transfers between devices: 95.8 us -> none  [local(): lax.psum_scatter(partial_rows, 'col', scatter_dimension=0, tiled=True)]
    pallas_call x0 -> x1, Pallas kernels: none -> 94.6 us  [local(): pl.pallas_call(kernel, out_shape=(jax.ShapeDtypeStruct(panel.shape, BF16)...]
    all_gather x1 -> x0, waiting for transfers between devices: 48.6 us -> none  [local(): col_block = lax.all_gather(moved, 'row', axis=0, tiled=True)]
    dot_general x3 -> x0, matrix products: 13.5 us -> none  [the longest x1 10.5 us: local(): jnp.dot(ancestor_inverse, col_block, preferred_element_type=jnp.float32)]
    ppermute x1 -> x0, starting transfers between devices: 6.28 us -> none  [local(): moved = lax.ppermute(masked, ('row', 'col'), flip)]
  transfers between devices with their start and end apart: 4 -> 0, of which waited for: 4 -> 0; matrix products, arithmetic and copies ran while one was open for 0% -> 0% of each run, Pallas kernels for 0% -> 0%
where the time goes in v2:
time: 98.8 us; the launch traced here: 98.6 us
  Pallas kernels  94.6 us (96%)
  local copies, waits for them, and re-layouts  3.44 us (3%)
    pallas_call x1, Pallas kernels, local(): pl.pallas_call(kernel, out_shape=(jax.ShapeDtypeStruct(panel.shape, BF16)...  94.6 us
    unnamed x2, local copies, waits for them, and re-layouts  3.44 us

profile of v2, /device:TPU:1, one launch (start us, length us, event | category | flops | bytes accessed | tf_op | source)
XLA Modules:
  0.0 98.6 jit_solution(3868577372169080196)
XLA Ops:
  0.6 94.6 %shard_map.59 = (bf16[128,512]{1,0:T(8,128)(2,1)}, f32[2,256,256]{2,1,0:T(8,128)}) custom-call(bf16[2048,2048]{1,0:T(8,128)(2,1)} %a_hbm.1, bf16[128,512]{1,0:T(8,128)(2,1)} %panel_ref.1, s32[2,128]{1,0:T(2,128)} %structure_ref.1, f32[2,256,256]{2,1,0:T(8,128)} %dinv_hbm.1), custom_call_target="tpu_custom_call" | custom-call | tf_op jit(solution)/shard_map/pallas_call | solution.py:328
  95.2 1.6 %copy.8 = bf16[128,512]{1,0:T(8,128)(2,1)} copy(bf16[128,512]{1,0:T(8,128)(2,1)} %get-tuple-element.4) | data formatting | bytes 262144
  96.8 1.9 %copy.9 = f32[2,256,256]{2,1,0:T(8,128)} copy(f32[2,256,256]{2,1,0:T(8,128)} %get-tuple-element.5) | data formatting | bytes 1048576

commit v3 on v2

v3 whole, which is shorter than its diff:
```python
import functools

import jax
import jax.numpy as jnp
from jax import lax
from jax.experimental import pallas as pl
from jax.experimental.pallas import tpu as pltpu
from jax.sharding import PartitionSpec as P

MESH = pl.DeviceIdType.MESH
F32 = jnp.float32
BF16 = jnp.bfloat16
I16 = jnp.int16
WIDE = 256
PIECE = 128
ROUND = 12582912.0


def encode(tile, ref):
    rows = tile.shape[0]
    top = jnp.maximum(jnp.max(jnp.abs(tile), axis=0, keepdims=True), 1e-30)
    power = jnp.floor(jnp.log2(top)) - 13.0
    scaled = tile * jnp.exp2(-power)
    whole = (scaled + ROUND) - ROUND
    ref[0:rows, :] = whole.astype(jnp.int32).astype(I16)
    ref[rows:rows + 16, :] = jnp.broadcast_to(power, (16, tile.shape[1])).astype(jnp.int32).astype(I16)


def decode(ref, first=0, count=None):
    rows = ref.shape[0] - 16
    count = rows if count is None else count
    power = ref[rows:rows + 16, :].astype(jnp.int32).astype(F32)
    scale = jnp.exp2(power)[0:1, :]
    return ref[first:first + count, :].astype(jnp.int32).astype(F32) * scale


def kernel(a_hbm, panel_ref, structure_ref, dinv_hbm, upper_ref, diag_ref,
           a_v, own, neg, xb, mg, sy, ry, sz, rz, ss, dsend, drecv, xs, xr, zr,
           dg, dchunk, lsem, ssem, rsem):
    R = lax.axis_index("row")
    C = lax.axis_index("col")
    x, zl, k = R // 4, (R // 2) % 2, R % 2
    y, zh = C // 4, C % 4
    z = zh * 2 + zl

    def at(dx=0, dy=0, dz=0, dzh=0, flip=False, sib=False):
        x2 = (x + dx) % 4
        y2 = (y + dy) % 4
        z2 = (z + dz + 2 * dzh) % 8
        zl2 = 1 - z2 % 2 if flip else z2 % 2
        k2 = 1 - k if sib else k
        return (x2 * 4 + zl2 * 2 + k2, y2 * 4 + z2 // 2)

    def holder(r, j):
        xs_, zls, ks = r // 4, (r // 2) % 2, r % 2
        i = (j % 4 - 2 * zls - ks + 8) % 4
        x2 = (2 * xs_ + 6 - j // 4) % 4
        upper_half = i // 2
        zl2 = jnp.where(zls == 0, (i + 1) // 2 % 2, 1 - upper_half)
        k2 = jnp.where(zls == 0, upper_half, i % 2)
        return x2 * 4 + zl2 * 2 + k2

    def piece(r, h):
        xs_, zls, ks = r // 4, (r // 2) % 2, r % 2
        x2, zl2, k2 = h // 4, (h // 2) % 2, h % 2
        i = jnp.where(zls == 0, jnp.where(zl2 == 0, 3 * k2, 1 + k2), 2 * (1 - zl2) + k2)
        return (2 * xs_ + 6 - x2) % 4 * 4 + (i + 2 * zls + ks) % 4

    ids = {}
    sends = []

    def copy(name, src, dst, dev):
        i = ids.setdefault(name, len(ids))
        return pltpu.make_async_remote_copy(
            src_ref=src, dst_ref=dst, send_sem=ssem.at[i], recv_sem=rsem.at[i],
            device_id=dev, device_id_type=MESH)

    def send(name, src, dst, dev):
        cp = copy(name, src, dst, dev)
        cp.start()
        sends.append(cp)

    def recv(name, dst):
        copy(name, dst, dst, at(sib=True)).wait_recv()

    loads = []
    for t in range(8):
        cp = pltpu.make_async_copy(a_hbm.at[pl.ds(t * 256, 256), :], a_v.at[pl.ds(t * 256, 256), :], lsem.at[t])
        cp.start()
        loads.append(cp)
    mine8 = pl.multiple_of(k * 128 + x * 32 + y * 8, 8)
    cp = pltpu.make_async_copy(dinv_hbm.at[:, pl.ds(mine8, 8), :], dchunk, lsem.at[8])
    cp.start()
    loads.append(cp)

    block = (R * 16 + C) // 2
    keeps = []
    for q in range(2):
        keep = structure_ref[q, block].astype(F32)
        keeps.append(keep)
        m = panel_ref[:, q * WIDE:(q + 1) * WIDE].astype(F32) * keep
        own[q] = m.astype(BF16)
        neg[q] = (-m).astype(BF16)

    barrier = pltpu.get_barrier_semaphore()
    target = (holder(R, C), R)
    source = (C, piece(C, R))
    partners = [at(sib=True), source]
    plane = [(d // 4, d % 4) for d in range(1, 16)]
    partners += [at(dx=dx, dy=dy) for dx, dy in plane]
    partners += [at(dx=d, flip=True) for d in (1, 3)]
    partners += [at(dz=d) for d in range(1, 8)]
    for dev in partners:
        pl.semaphore_signal(barrier, inc=1, device_id=dev, device_id_type=MESH)
    pl.semaphore_wait(barrier, len(partners))

    def slot(q, s):
        return xb.at[q, pl.ds(pl.multiple_of(s * PIECE, PIECE), PIECE), :]

    def half(q, s, h):
        return xb.at[q, pl.ds(pl.multiple_of(s * PIECE + h * 64, 64), 64), :]

    def lane(dx, n, other=False):
        return piece(C, ((x + dx) % 4) * 4 + (zl + n) % 2 * 2 + (1 - k if other else k))

    for q in range(2):
        send(("g1", q), neg.at[q], slot(q, C), target)

    def share(q, s, i):
        send(("gs", q, i), slot(q, s), slot(q, s), at(sib=True))

    def s1(q):
        s = lane(0, 0)
        recv(("g1", q), slot(q, s))
        names = [("xp", at(dx=1)), ("xm", at(dx=-1)), ("z", at(flip=True))]
        if q == 0:
            names += [("zp", at(dx=1, flip=True)), ("zm", at(dx=-1, flip=True))]
        for name, dev in names:
            send((name, q), slot(q, s), slot(q, s), dev)
        share(q, s, 0)

    def s2(q):
        s = lane(0, 1)
        recv(("z", q), slot(q, s))
        if q == 1:
            send(("zp", q), slot(q, s), slot(q, s), at(dx=1))
            send(("zm", q), slot(q, s), slot(q, s), at(dx=-1))
        share(q, s, 1)

    def s3(q, n):
        s = lane(1, n)
        recv(("zm" if n else "xm", q), slot(q, s))
        send(("hm", q, n), half(q, s, 0), half(q, s, 0), at(dx=-1))
        share(q, s, 2 + n)
        s = lane(-1, n)
        recv(("zp" if n else "xp", q), slot(q, s))
        send(("hp", q, n), half(q, s, 1), half(q, s, 1), at(dx=1))
        share(q, s, 4 + n)

    def s5(q, n):
        s = lane(2, n)
        recv(("hm", q, n), half(q, s, 0))
        recv(("hp", q, n), half(q, s, 1))
        share(q, s, 6 + n)

    def s6(q):
        for n in range(2):
            for i, dx in ((0, 0), (2, 1), (4, -1), (6, 2)):
                recv(("gs", q, i + n), slot(q, lane(dx, n, True)))

    def m_rows(d):
        return mg.at[:, pl.ds(pl.multiple_of(((zh + d) % 4) * PIECE, PIECE), PIECE), :]

    def m_send():
        for q in range(2):
            mg[q, pl.ds(pl.multiple_of(zh * PIECE, PIECE), PIECE), :] = own[q]
        for d in (1, 2, 3):
            send(("m", d), own, m_rows(0), at(dzh=d))

    def m_recv():
        for d in (1, 2, 3):
            recv(("m", d), m_rows(4 - d))

    def tile(q, dy, u):
        r0 = pl.multiple_of(((y + dy) % 4) * 512 + u * 256, 256)
        return jnp.dot(a_v[pl.ds(r0, 256), :], xb[q], preferred_element_type=F32)

    def y_send(q, i, value, dy):
        encode(value, sy.at[q, i])
        send(("y", q, i), sy.at[q, i], ry.at[q, i], at(dy=dy))

    def y_first(q, after):
        y_send(q, 0, tile(q, 2, 0), 1)
        after(0)
        y_send(q, 1, tile(q, 2, 1), -1)
        after(1)
        y_send(q, 2, tile(q, 1, 1), 1)
        y_send(q, 3, tile(q, -1, 0), -1)

    def y_own(q):
        for u in range(2):
            ss[q, u * 256:(u + 1) * 256, :] = tile(q, 0, u)

    def y_relay(q):
        t = tile(q, 1, 0)
        recv(("y", q, 0), ry.at[q, 0])
        y_send(q, 4, t + decode(ry.at[q, 0]), 1)
        t = tile(q, -1, 1)
        recv(("y", q, 1), ry.at[q, 1])
        y_send(q, 5, t + decode(ry.at[q, 1]), -1)

    def y_last(q):
        for i in (2, 3, 4, 5):
            recv(("y", q, i), ry.at[q, i])
        ss[q, 0:256, :] = ss[q, 0:256, :] + decode(ry.at[q, 3]) + decode(ry.at[q, 4])
        ss[q, 256:512, :] = ss[q, 256:512, :] + decode(ry.at[q, 2]) + decode(ry.at[q, 5])

    def z_ref(buf, q, i):
        return buf.at[q, i, pl.ds(0, 80 if i < 2 else 144), :]

    def z_send(q, i, value, dzh):
        encode(value, z_ref(sz, q, i))
        send(("z", q, i), z_ref(sz, q, i), z_ref(rz, q, i), at(dzh=dzh))

    def z_rows(q, d, start, count):
        r0 = pl.multiple_of(((zh + d) % 4) * PIECE + start, 64)
        return ss[q, pl.ds(r0, count), :]

    def z_first(q):
        z_send(q, 0, z_rows(q, 2, 0, 64), 1)
        z_send(q, 1, z_rows(q, 2, 64, 64), -1)

    def z_relay(q):
        recv(("z", q, 0), z_ref(rz, q, 0))
        v = jnp.concatenate([z_rows(q, 1, 0, 64) + decode(z_ref(rz, q, 0)), z_rows(q, 1, 64, 64)], axis=0)
        z_send(q, 2, v, 1)
        recv(("z", q, 1), z_ref(rz, q, 1))
        v = jnp.concatenate([z_rows(q, -1, 0, 64), z_rows(q, -1, 64, 64) + decode(z_ref(rz, q, 1))], axis=0)
        z_send(q, 3, v, -1)

    def z_last(q):
        recv(("z", q, 2), z_ref(rz, q, 2))
        recv(("z", q, 3), z_ref(rz, q, 3))
        full = z_rows(q, 0, 0, PIECE) + decode(z_ref(rz, q, 2)) + decode(z_ref(rz, q, 3))
        upper_ref[:, q * WIDE:(q + 1) * WIDE] = (full * keeps[q]).astype(BF16)

    mate = at(sib=True)

    def rows(start, count):
        return pl.ds(pl.multiple_of(start, 8), count)

    def d_core(q):
        dims = (((0,), (0,)), ((), ()))
        part = ss[q]
        high = part.astype(BF16)
        low = (part - high.astype(F32)).astype(BF16)
        dsend[q] = (lax.dot_general(mg[q], high, dims, preferred_element_type=F32)
                    + lax.dot_general(mg[q], low, dims, preferred_element_type=F32))
        send(("core", q), dsend.at[q, rows((1 - k) * 128, 128), :], drecv.at[q], mate)

    def d_plane(q):
        recv(("core", q), drecv.at[q])
        xs[q] = dsend[q, rows(k * 128, 128), :] + drecv[q]
        for i, (dx, dy) in enumerate(plane):
            r0 = ((x + dx) % 4) * 32 + ((y + dy) % 4) * 8
            send(("dp", q, i), xs.at[q, rows(r0, 8), :], xr.at[q, i], at(dx=dx, dy=dy))

    def d_z(q):
        total = xs[q, rows(x * 32 + y * 8, 8), :]
        for i in range(15):
            recv(("dp", q, i), xr.at[q, i])
            total = total + xr[q, i]
        zr[q, z] = total
        for d in range(1, 8):
            send(("dz", q, d), zr.at[q, z], zr.at[q, z], at(dz=d))

    def d_back(q):
        for d in range(1, 8):
            recv(("dz", q, d), zr.at[q, (z + 8 - d) % 8])
        total = zr[q, 0]
        for i in range(1, 8):
            total = total + zr[q, i]
        dg[q, pl.ds(mine8, 8), :] = dchunk[q] - total
        part = dg.at[q, pl.ds(mine8, 8), :]
        for i, (dx, dy) in enumerate(plane):
            send(("ap", q, i), part, part, at(dx=dx, dy=dy))

    def d_back_core(q):
        for i, (dx, dy) in enumerate(plane):
            r0 = k * 128 + ((x + 4 - dx) % 4) * 32 + ((y + 4 - dy) % 4) * 8
            recv(("ap", q, i), dg.at[q, rows(r0, 8), :])
        part = dg.at[q, rows(k * 128, 128), :]
        send(("ac", q), part, part, mate)

    def d_end(q):
        recv(("ac", q), dg.at[q, rows((1 - k) * 128, 128), :])
        diag_ref[q] = dg[q]

    s1(0)
    s1(1)
    s3(0, 0)
    s2(1)
    s3(0, 1)
    s2(0)
    s3(1, 0)
    for cp in loads:
        cp.wait()
    s5(0, 0)
    s3(1, 1)
    s5(0, 1)
    s6(0)
    y_first(0, lambda i: m_send() if i == 0 else s5(1, 0))
    y_own(0)
    s5(1, 1)
    y_relay(0)
    s6(1)
    y_first(1, lambda i: None)
    y_own(1)
    m_recv()
    y_last(0)
    d_core(0)
    z_first(0)
    y_relay(1)
    d_plane(0)
    z_relay(0)
    z_last(0)
    d_z(0)
    y_last(1)
    d_core(1)
    z_first(1)
    d_plane(1)
    d_back(0)
    z_relay(1)
    d_z(1)
    z_last(1)
    d_back_core(0)
    d_back(1)
    d_end(0)
    d_back_core(1)
    d_end(1)
    for cp in sends:
        cp.wait_send()
    assert len(ids) <= COPIES, len(ids)


def place(upper_ref, diag_ref, upper_out, diag_out):
    upper_out[...] = upper_ref[...]
    diag_out[...] = diag_ref[...]


COPIES = 160


def local(ancestor_inverse, panel, structure, diag_inverse):
    vmem = pl.BlockSpec(memory_space=pltpu.VMEM)
    hbm = pl.BlockSpec(memory_space=pltpu.HBM)
    upper, diagonal = pl.pallas_call(
        kernel,
        out_shape=(jax.ShapeDtypeStruct(panel.shape, BF16), jax.ShapeDtypeStruct(diag_inverse.shape, F32)),
        in_specs=[hbm, vmem, pl.BlockSpec(memory_space=pltpu.SMEM), hbm],
        out_specs=(vmem, vmem),
        scratch_shapes=[
            pltpu.VMEM((2048, 2048), BF16),
            pltpu.VMEM((2, PIECE, WIDE), BF16),
            pltpu.VMEM((2, PIECE, WIDE), BF16),
            pltpu.VMEM((2, 2048, WIDE), BF16),
            pltpu.VMEM((2, 512, WIDE), BF16),
            pltpu.VMEM((2, 6, 272, WIDE), I16),
            pltpu.VMEM((2, 6, 272, WIDE), I16),
            pltpu.VMEM((2, 4, 144, WIDE), I16),
            pltpu.VMEM((2, 4, 144, WIDE), I16),
            pltpu.VMEM((2, 512, WIDE), F32),
            pltpu.VMEM((2, WIDE, WIDE), F32),
            pltpu.VMEM((2, 128, WIDE), F32),
            pltpu.VMEM((2, 128, WIDE), F32),
            pltpu.VMEM((2, 15, 8, WIDE), F32),
            pltpu.VMEM((2, 8, 8, WIDE), F32),
            pltpu.VMEM((2, WIDE, WIDE), F32),
            pltpu.VMEM((2, 8, WIDE), F32),
            pltpu.SemaphoreType.DMA((9,)),
            pltpu.SemaphoreType.DMA((COPIES,)),
            pltpu.SemaphoreType.DMA((COPIES,)),
        ],
        compiler_params=pltpu.CompilerParams(
            collective_id=0, has_side_effects=True, vmem_limit_bytes=57 * 1024 * 1024),
    )(ancestor_inverse, panel, structure, diag_inverse)
    return pl.pallas_call(
        place,
        out_shape=(jax.ShapeDtypeStruct(upper.shape, BF16), jax.ShapeDtypeStruct(diagonal.shape, F32)),
        in_specs=[vmem, vmem],
        out_specs=(vmem, vmem),
        compiler_params=pltpu.CompilerParams(vmem_limit_bytes=4 * 1024 * 1024),
    )(upper, diagonal)


def solution(mesh):
    return jax.shard_map(
        local,
        mesh=mesh,
        in_specs=(P("row", "col"), P(("row", "col"), None), P(), P()),
        out_specs=(P(("row", "col"), None), P()),
        check_vma=False,
    )
```

time: 98.8 us -> 82 us (0.83)
  Pallas kernels: 94.6 us -> 79.2 us
  local copies, waits for them, and re-layouts: 3.44 us -> 1.94 us
    pallas_call x1, Pallas kernels: 94.6 us -> 78.3 us  [local(): pl.pallas_call(kernel, out_shape=(jax.ShapeDtypeStruct(panel.shape, BF16)...]
    unnamed x2 -> x4, local copies, waits for them, and re-layouts: 3.44 us -> 1.94 us
where the time goes in v3:
time: 82 us; the launch traced here: 81.8 us
  Pallas kernels  79.2 us (97%)
  local copies, waits for them, and re-layouts  1.94 us (2%)
    pallas_call x1, Pallas kernels, local(): pl.pallas_call(kernel, out_shape=(jax.ShapeDtypeStruct(panel.shape, BF16)...  78.3 us
    unnamed x4, local copies, waits for them, and re-layouts  1.94 us

profile of v3, /device:TPU:1, one launch (start us, length us, event | category | flops | bytes accessed | tf_op | source)
XLA Modules:
  0.0 81.8 jit_solution(3213986623421109044)
XLA Ops:
  0.6 78.3 %shard_map.59 = (bf16[128,512]{1,0:T(8,128)(2,1)}, f32[2,256,256]{2,1,0:T(8,128)}) custom-call(bf16[2048,2048]{1,0:T(8,128)(2,1)} %a_hbm.1, bf16[128,512]{1,0:T(8,128)(2,1)} %panel_ref.1, s32[2,128]{1,0:T(2,128)} %structure_ref.1, f32[2,256,256]{2,1,0:T(8,128)} %dinv_hbm.1), custom_call_target="tpu_custom_call" | custom-call | tf_op jit(solution)/shard_map/pallas_call | solution.py:357
  79.0 0.0 copy-start
  79.0 1.0 %copy-done = f32[2,256,256]{2,1,0:T(8,128)S(1)} copy-done((f32[2,256,256]{2,1,0:T(8,128)S(1)}, f32[2,256,256]{2,1,0:T(8,128)}, u32[]{:S(2)}) %copy-start) | copy-done | bytes 524312
  80.0 0.0 copy-start.1
  80.0 0.9 %copy-done.1 = bf16[128,512]{1,0:T(8,128)(2,1)S(1)} copy-done((bf16[128,512]{1,0:T(8,128)(2,1)S(1)}, bf16[128,512]{1,0:T(8,128)(2,1)}, u32[]{:S(2)}) %copy-start.1) | copy-done | bytes 131096
  80.9 0.9 %shard_map.60 = (bf16[128,512]{1,0:T(8,128)(2,1)}, f32[2,256,256]{2,1,0:T(8,128)}) custom-call(bf16[128,512]{1,0:T(8,128)(2,1)S(1)} %copy-done.1, f32[2,256,256]{2,1,0:T(8,128)S(1)} %copy-done), custom_call_target="tpu_custom_call" | custom-call | tf_op jit(solution)/shard_map/pallas_call | solution.py:387
Async XLA Ops:
  79.0 1.0 %copy-start = (f32[2,256,256]{2,1,0:T(8,128)S(1)}, f32[2,256,256]{2,1,0:T(8,128)}, u32[]{:S(2)}) copy-start(f32[2,256,256]{2,1,0:T(8,128)} %get-tuple-element.5.diag_ref) | copy-start | bytes 1572868
  80.0 0.9 %copy-start.1 = (bf16[128,512]{1,0:T(8,128)(2,1)S(1)}, bf16[128,512]{1,0:T(8,128)(2,1)}, u32[]{:S(2)}) copy-start(bf16[128,512]{1,0:T(8,128)(2,1)} %get-tuple-element.4.upper_ref) | copy-start | bytes 393220

commit v4 on v3

--- a/solution.py
+++ b/solution.py
@@ -34,9 +34,9 @@
     return ref[first:first + count, :].astype(jnp.int32).astype(F32) * scale
 
 
-def kernel(a_hbm, panel_ref, structure_ref, dinv_hbm, upper_ref, diag_ref,
+def kernel(a_hbm, panel_ref, structure_ref, upper_ref, diag_ref,
            a_v, own, neg, xb, mg, sy, ry, sz, rz, ss, dsend, drecv, xs, xr, zr,
-           dg, dchunk, lsem, ssem, rsem):
+           dg, lsem, ssem, rsem):
     R = lax.axis_index("row")
     C = lax.axis_index("col")
     x, zl, k = R // 4, (R // 2) % 2, R % 2
@@ -83,15 +83,25 @@
     def recv(name, dst):
         copy(name, dst, dst, at(sib=True)).wait_recv()
 
+    barrier = pltpu.get_barrier_semaphore()
+    target = (holder(R, C), R)
+    source = (C, piece(C, R))
+    plane = sorted(((d // 4, d % 4) for d in range(1, 16)),
+                   key=lambda d: -min(d[0], 4 - d[0]) - min(d[1], 4 - d[1]))
+    along = (4, 3, 5, 2, 6, 1, 7)
+    partners = [source] + [at(dz=d) for d in along[:3]]
+    partners += [at(dx=dx, dy=dy) for dx, dy in plane]
+    partners += [at(dz=d) for d in along[3:]]
+    partners += [at(dx=d, flip=True) for d in (1, 3)]
+    partners += [at(sib=True)]
+    for dev in partners:
+        pl.semaphore_signal(barrier, inc=1, device_id=dev, device_id_type=MESH)
     loads = []
     for t in range(8):
         cp = pltpu.make_async_copy(a_hbm.at[pl.ds(t * 256, 256), :], a_v.at[pl.ds(t * 256, 256), :], lsem.at[t])
         cp.start()
         loads.append(cp)
     mine8 = pl.multiple_of(k * 128 + x * 32 + y * 8, 8)
-    cp = pltpu.make_async_copy(dinv_hbm.at[:, pl.ds(mine8, 8), :], dchunk, lsem.at[8])
-    cp.start()
-    loads.append(cp)
 
     block = (R * 16 + C) // 2
     keeps = []
@@ -102,16 +112,6 @@
         own[q] = m.astype(BF16)
         neg[q] = (-m).astype(BF16)
 
-    barrier = pltpu.get_barrier_semaphore()
-    target = (holder(R, C), R)
-    source = (C, piece(C, R))
-    partners = [at(sib=True), source]
-    plane = [(d // 4, d % 4) for d in range(1, 16)]
-    partners += [at(dx=dx, dy=dy) for dx, dy in plane]
-    partners += [at(dx=d, flip=True) for d in (1, 3)]
-    partners += [at(dz=d) for d in range(1, 8)]
-    for dev in partners:
-        pl.semaphore_signal(barrier, inc=1, device_id=dev, device_id_type=MESH)
     pl.semaphore_wait(barrier, len(partners))
 
     def slot(q, s):
@@ -123,7 +123,7 @@
     def lane(dx, n, other=False):
         return piece(C, ((x + dx) % 4) * 4 + (zl + n) % 2 * 2 + (1 - k if other else k))
 
-    for q in range(2):
+    def g1(q):
         send(("g1", q), neg.at[q], slot(q, C), target)
 
     def share(q, s, i):
@@ -132,9 +132,10 @@
     def s1(q):
         s = lane(0, 0)
         recv(("g1", q), slot(q, s))
-        names = [("xp", at(dx=1)), ("xm", at(dx=-1)), ("z", at(flip=True))]
+        names = [("xp", at(dx=1)), ("xm", at(dx=-1))]
         if q == 0:
             names += [("zp", at(dx=1, flip=True)), ("zm", at(dx=-1, flip=True))]
+        names += [("z", at(flip=True))]
         for name, dev in names:
             send((name, q), slot(q, s), slot(q, s), dev)
         share(q, s, 0)
@@ -174,7 +175,7 @@
     def m_send():
         for q in range(2):
             mg[q, pl.ds(pl.multiple_of(zh * PIECE, PIECE), PIECE), :] = own[q]
-        for d in (1, 2, 3):
+        for d in (2, 1, 3):
             send(("m", d), own, m_rows(0), at(dzh=d))
 
     def m_recv():
@@ -271,7 +272,7 @@
             recv(("dp", q, i), xr.at[q, i])
             total = total + xr[q, i]
         zr[q, z] = total
-        for d in range(1, 8):
+        for d in along:
             send(("dz", q, d), zr.at[q, z], zr.at[q, z], at(dz=d))
 
     def d_back(q):
@@ -280,7 +281,7 @@
         total = zr[q, 0]
         for i in range(1, 8):
             total = total + zr[q, i]
-        dg[q, pl.ds(mine8, 8), :] = dchunk[q] - total
+        dg[q, pl.ds(mine8, 8), :] = total
         part = dg.at[q, pl.ds(mine8, 8), :]
         for i, (dx, dy) in enumerate(plane):
             send(("ap", q, i), part, part, at(dx=dx, dy=dy))
@@ -296,23 +297,25 @@
         recv(("ac", q), dg.at[q, rows((1 - k) * 128, 128), :])
         diag_ref[q] = dg[q]
 
+    g1(0)
     s1(0)
-    s1(1)
+    g1(1)
     s3(0, 0)
-    s2(1)
     s3(0, 1)
     s2(0)
-    s3(1, 0)
+    s5(0, 0)
+    s1(1)
+    s5(0, 1)
     for cp in loads:
         cp.wait()
-    s5(0, 0)
+    s6(0)
+    y_first(0, lambda i: m_send() if i else s2(1))
+    s3(1, 0)
+    y_own(0)
     s3(1, 1)
-    s5(0, 1)
-    s6(0)
-    y_first(0, lambda i: m_send() if i == 0 else s5(1, 0))
-    y_own(0)
+    y_relay(0)
+    s5(1, 0)
     s5(1, 1)
-    y_relay(0)
     s6(1)
     y_first(1, lambda i: None)
     y_own(1)
@@ -323,17 +326,17 @@
     y_relay(1)
     d_plane(0)
     z_relay(0)
-    z_last(0)
     d_z(0)
     y_last(1)
     d_core(1)
     z_first(1)
+    z_last(0)
     d_plane(1)
     d_back(0)
+    d_z(1)
     z_relay(1)
-    d_z(1)
+    d_back_core(0)
     z_last(1)
-    d_back_core(0)
     d_back(1)
     d_end(0)
     d_back_core(1)
@@ -343,9 +346,9 @@
     assert len(ids) <= COPIES, len(ids)
 
 
-def place(upper_ref, diag_ref, upper_out, diag_out):
+def place(upper_ref, update_ref, dinv_ref, upper_out, diag_out):
     upper_out[...] = upper_ref[...]
-    diag_out[...] = diag_ref[...]
+    diag_out[...] = dinv_ref[...] - update_ref[...]
 
 
 COPIES = 160
@@ -354,10 +357,10 @@
 def local(ancestor_inverse, panel, structure, diag_inverse):
     vmem = pl.BlockSpec(memory_space=pltpu.VMEM)
     hbm = pl.BlockSpec(memory_space=pltpu.HBM)
-    upper, diagonal = pl.pallas_call(
+    upper, update = pl.pallas_call(
         kernel,
         out_shape=(jax.ShapeDtypeStruct(panel.shape, BF16), jax.ShapeDtypeStruct(diag_inverse.shape, F32)),
-        in_specs=[hbm, vmem, pl.BlockSpec(memory_space=pltpu.SMEM), hbm],
+        in_specs=[hbm, vmem, pl.BlockSpec(memory_space=pltpu.SMEM)],
         out_specs=(vmem, vmem),
         scratch_shapes=[
             pltpu.VMEM((2048, 2048), BF16),
@@ -376,21 +379,20 @@
             pltpu.VMEM((2, 15, 8, WIDE), F32),
             pltpu.VMEM((2, 8, 8, WIDE), F32),
             pltpu.VMEM((2, WIDE, WIDE), F32),
-            pltpu.VMEM((2, 8, WIDE), F32),
-            pltpu.SemaphoreType.DMA((9,)),
+            pltpu.SemaphoreType.DMA((8,)),
             pltpu.SemaphoreType.DMA((COPIES,)),
             pltpu.SemaphoreType.DMA((COPIES,)),
         ],
         compiler_params=pltpu.CompilerParams(
-            collective_id=0, has_side_effects=True, vmem_limit_bytes=57 * 1024 * 1024),
-    )(ancestor_inverse, panel, structure, diag_inverse)
+            collective_id=0, has_side_effects=True, vmem_limit_bytes=52 * 1024 * 1024),
+    )(ancestor_inverse, panel, structure)
     return pl.pallas_call(
         place,
-        out_shape=(jax.ShapeDtypeStruct(upper.shape, BF16), jax.ShapeDtypeStruct(diagonal.shape, F32)),
-        in_specs=[vmem, vmem],
+        out_shape=(jax.ShapeDtypeStruct(upper.shape, BF16), jax.ShapeDtypeStruct(update.shape, F32)),
+        in_specs=[vmem, vmem, vmem],
         out_specs=(vmem, vmem),
         compiler_params=pltpu.CompilerParams(vmem_limit_bytes=4 * 1024 * 1024),
-    )(upper, diagonal)
+    )(upper, update, diag_inverse)
 
 
 def solution(mesh):

time: 82 us -> 77.9 us (0.950)
  Pallas kernels: 79.2 us -> 75.5 us
    pallas_call x1, Pallas kernels: 78.3 us -> 74.6 us  [local(): pl.pallas_call(kernel, out_shape=(jax.ShapeDtypeStruct(panel.shape, BF16)...]
    unnamed x4 -> x6, local copies, waits for them, and re-layouts: 1.94 us -> 1.64 us
where the time goes in v4:
time: 77.9 us; the launch traced here: 77.8 us
  Pallas kernels  75.5 us (97%)
  local copies, waits for them, and re-layouts  1.64 us (2%)
    pallas_call x1, Pallas kernels, local(): pl.pallas_call(kernel, out_shape=(jax.ShapeDtypeStruct(panel.shape, BF16)...  74.6 us
    unnamed x6, local copies, waits for them, and re-layouts  1.64 us

profile of v4, /device:TPU:1, one launch (start us, length us, event | category | flops | bytes accessed | tf_op | source)
XLA Modules:
  0.0 77.8 jit_solution(9229377005347247942)
XLA Ops:
  0.6 0.0 copy-start
  0.6 0.0 copy-start.1
  0.7 1.0 %copy-done.1 = bf16[128,512]{1,0:T(8,128)(2,1)S(1)} copy-done((bf16[128,512]{1,0:T(8,128)(2,1)S(1)}, bf16[128,512]{1,0:T(8,128)(2,1)}, u32[]{:S(2)}) %copy-start.1) | copy-done | bytes 131096
  1.6 0.0 copy-start.2
  1.6 0.7 copy-done.2
  2.3 74.6 %shard_map.59 = (bf16[128,512]{1,0:T(8,128)(2,1)S(1)}, f32[2,256,256]{2,1,0:T(8,128)S(1)}) custom-call(bf16[2048,2048]{1,0:T(8,128)(2,1)} %a_hbm.1, bf16[128,512]{1,0:T(8,128)(2,1)S(1)} %copy-done.1, s32[2,128]{1,0:T(2,128)S(1)} %copy-done.2), custom_call_target="tpu_custom_call" | custom-call | tf_op jit(solution)/shard_map/pallas_call | solution.py:360
  76.9 0.0 copy-done
  76.9 0.9 %shard_map.60 = (bf16[128,512]{1,0:T(8,128)(2,1)}, f32[2,256,256]{2,1,0:T(8,128)}) custom-call(bf16[128,512]{1,0:T(8,128)(2,1)S(1)} %get-tuple-element.4.upper_ref, f32[2,256,256]{2,1,0:T(8,128)S(1)} %get-tuple-element.5.update_ref, f32[2,256,256]{2,1,0:T(8,128)S(1)} %copy-done), custom_call_target="tpu_custom_call" | custom-call | tf_op jit(solution)/shard_map/pallas_call | solution.py:389
Async XLA Ops:
  0.6 76.3 %copy-start = (f32[2,256,256]{2,1,0:T(8,128)S(1)}, f32[2,256,256]{2,1,0:T(8,128)}, u32[]{:S(2)}) copy-start(f32[2,256,256]{2,1,0:T(8,128)} %dinv_ref.1) | copy-start | bytes 1572868
  0.6 1.0 %copy-start.1 = (bf16[128,512]{1,0:T(8,128)(2,1)S(1)}, bf16[128,512]{1,0:T(8,128)(2,1)}, u32[]{:S(2)}) copy-start(bf16[128,512]{1,0:T(8,128)(2,1)} %panel_ref.1) | copy-start | bytes 393220
  1.6 0.7 copy-start.2

commit v5 on v4

--- a/solution.py
+++ b/solution.py
@@ -330,16 +330,16 @@
     y_last(1)
     d_core(1)
     z_first(1)
+    d_plane(1)
     z_last(0)
-    d_plane(1)
     d_back(0)
     d_z(1)
     z_relay(1)
     d_back_core(0)
-    z_last(1)
     d_back(1)
     d_end(0)
     d_back_core(1)
+    z_last(1)
     d_end(1)
     for cp in sends:
         cp.wait_send()

time: 77.9 us -> 76.6 us (0.983)
  Pallas kernels: 75.5 us -> 74.2 us
    pallas_call x1, Pallas kernels: 74.6 us -> 73.3 us  [local(): pl.pallas_call(kernel, out_shape=(jax.ShapeDtypeStruct(panel.shape, BF16)...]
where the time goes in v5:
time: 76.6 us; the launch traced here: 76.5 us
  Pallas kernels  74.2 us (97%)
  local copies, waits for them, and re-layouts  1.64 us (2%)
    pallas_call x1, Pallas kernels, local(): pl.pallas_call(kernel, out_shape=(jax.ShapeDtypeStruct(panel.shape, BF16)...  73.3 us
    unnamed x6, local copies, waits for them, and re-layouts  1.64 us

profile of v5, /device:TPU:1, one launch (start us, length us, event | category | flops | bytes accessed | tf_op | source)
XLA Modules:
  0.0 76.5 jit_solution(6157175746901104096)
XLA Ops:
  0.6 0.0 copy-start
  0.6 0.0 copy-start.1
  0.7 1.0 %copy-done.1 = bf16[128,512]{1,0:T(8,128)(2,1)S(1)} copy-done((bf16[128,512]{1,0:T(8,128)(2,1)S(1)}, bf16[128,512]{1,0:T(8,128)(2,1)}, u32[]{:S(2)}) %copy-start.1) | copy-done | bytes 131096
  1.6 0.0 copy-start.2
  1.6 0.7 copy-done.2
  2.3 73.3 %shard_map.59 = (bf16[128,512]{1,0:T(8,128)(2,1)S(1)}, f32[2,256,256]{2,1,0:T(8,128)S(1)}) custom-call(bf16[2048,2048]{1,0:T(8,128)(2,1)} %a_hbm.1, bf16[128,512]{1,0:T(8,128)(2,1)S(1)} %copy-done.1, s32[2,128]{1,0:T(2,128)S(1)} %copy-done.2), custom_call_target="tpu_custom_call" | custom-call | tf_op jit(solution)/shard_map/pallas_call | solution.py:360
  75.5 0.0 copy-done
  75.6 0.9 %shard_map.60 = (bf16[128,512]{1,0:T(8,128)(2,1)}, f32[2,256,256]{2,1,0:T(8,128)}) custom-call(bf16[128,512]{1,0:T(8,128)(2,1)S(1)} %get-tuple-element.4.upper_ref, f32[2,256,256]{2,1,0:T(8,128)S(1)} %get-tuple-element.5.update_ref, f32[2,256,256]{2,1,0:T(8,128)S(1)} %copy-done), custom_call_target="tpu_custom_call" | custom-call | tf_op jit(solution)/shard_map/pallas_call | solution.py:389
Async XLA Ops:
  0.6 74.9 %copy-start = (f32[2,256,256]{2,1,0:T(8,128)S(1)}, f32[2,256,256]{2,1,0:T(8,128)}, u32[]{:S(2)}) copy-start(f32[2,256,256]{2,1,0:T(8,128)} %dinv_ref.1) | copy-start | bytes 1572868
  0.6 1.0 %copy-start.1 = (bf16[128,512]{1,0:T(8,128)(2,1)S(1)}, bf16[128,512]{1,0:T(8,128)(2,1)}, u32[]{:S(2)}) copy-start(bf16[128,512]{1,0:T(8,128)(2,1)} %panel_ref.1) | copy-start | bytes 393220
  1.6 0.7 copy-start.2

commit v6 on v5

--- a/solution.py
+++ b/solution.py
@@ -302,9 +302,9 @@
     g1(1)
     s3(0, 0)
     s3(0, 1)
+    s1(1)
     s2(0)
     s5(0, 0)
-    s1(1)
     s5(0, 1)
     for cp in loads:
         cp.wait()

time: 76.6 us -> 76.1 us (level)
  no operation moved by 1% of the time
where the time goes in v6:
time: 76.1 us; the launch traced here: 76 us
  Pallas kernels  73.7 us (97%)
  local copies, waits for them, and re-layouts  1.64 us (2%)
    pallas_call x1, Pallas kernels, local(): pl.pallas_call(kernel, out_shape=(jax.ShapeDtypeStruct(panel.shape, BF16)...  72.8 us
    unnamed x6, local copies, waits for them, and re-layouts  1.64 us

profile of v6, /device:TPU:1, one launch (start us, length us, event | category | flops | bytes accessed | tf_op | source)
XLA Modules:
  0.0 76.0 jit_solution(6176714516938401995)
XLA Ops:
  0.6 0.0 copy-start
  0.6 0.0 copy-start.1
  0.7 1.0 %copy-done.1 = bf16[128,512]{1,0:T(8,128)(2,1)S(1)} copy-done((bf16[128,512]{1,0:T(8,128)(2,1)S(1)}, bf16[128,512]{1,0:T(8,128)(2,1)}, u32[]{:S(2)}) %copy-start.1) | copy-done | bytes 131096
  1.6 0.0 copy-start.2
  1.6 0.7 copy-done.2
  2.3 72.8 %shard_map.59 = (bf16[128,512]{1,0:T(8,128)(2,1)S(1)}, f32[2,256,256]{2,1,0:T(8,128)S(1)}) custom-call(bf16[2048,2048]{1,0:T(8,128)(2,1)} %a_hbm.1, bf16[128,512]{1,0:T(8,128)(2,1)S(1)} %copy-done.1, s32[2,128]{1,0:T(2,128)S(1)} %copy-done.2), custom_call_target="tpu_custom_call" | custom-call | tf_op jit(solution)/shard_map/pallas_call | solution.py:360
  75.1 0.0 copy-done
  75.1 0.9 %shard_map.60 = (bf16[128,512]{1,0:T(8,128)(2,1)}, f32[2,256,256]{2,1,0:T(8,128)}) custom-call(bf16[128,512]{1,0:T(8,128)(2,1)S(1)} %get-tuple-element.4.upper_ref, f32[2,256,256]{2,1,0:T(8,128)S(1)} %get-tuple-element.5.update_ref, f32[2,256,256]{2,1,0:T(8,128)S(1)} %copy-done), custom_call_target="tpu_custom_call" | custom-call | tf_op jit(solution)/shard_map/pallas_call | solution.py:389
Async XLA Ops:
  0.6 74.4 %copy-start = (f32[2,256,256]{2,1,0:T(8,128)S(1)}, f32[2,256,256]{2,1,0:T(8,128)}, u32[]{:S(2)}) copy-start(f32[2,256,256]{2,1,0:T(8,128)} %dinv_ref.1) | copy-start | bytes 1572868
  0.6 1.0 %copy-start.1 = (bf16[128,512]{1,0:T(8,128)(2,1)S(1)}, bf16[128,512]{1,0:T(8,128)(2,1)}, u32[]{:S(2)}) copy-start(bf16[128,512]{1,0:T(8,128)(2,1)} %panel_ref.1) | copy-start | bytes 393220
  1.6 0.7 copy-start.2
